TPU v7x, 32 devices: a whole 2x2x4 slice. The times are simulated.
32 devices in a mesh: bas: 8 (over y, x, core), aux: 4 (over z).
Axes of the slice: x: 2, y: 2, z: 4, core: 2. Of those that a mesh axis runs over, the one named last changes fastest.
Arguments:
- integrals: bfloat16 [4, 8192, 8192], P('aux', 'bas'), may hold values from -6 to 6
- screen: int32 [4, 64, 64], P('aux', 'bas'), may hold values from 0 to 1, as said below
- coefficients: bfloat16 [8192, 384], P('bas'), may hold values from -0.0625 to 0.0625
- weights: float32 [384], replicated, may hold values from -2 to 2
Outputs:
- exchange: bfloat16 [8192, 8192], P('aux', 'bas')
Inputs may be any that keep to these rules, and one draw needn't show every extreme that they name: `screen`: every block with equal row and column block index is 1; the share of ones differs from row block to row block.
All inputs are finite; a program needn't handle non-finite values.
Results may differ from a plain program's by a relative error of at most 0.018.
Values may be sent and summed in bfloat16 or wider, within the bound.
A program may use at most 128 MiB of HBM per device.

v0:
```python
import functools
import math

import jax
import jax.numpy as jnp
from jax import lax
from jax.experimental import pallas as pl
from jax.experimental.pallas import tpu as pltpu
from jax.sharding import PartitionSpec as P

BLOCK = 128
LANES = 128


def kernel(groups, aux, scale, integrals, screen, coefs, weights, out,
           ints, fac, acc, right, left, wt, total, result,
           load_sem, ring_send, ring_recv, pair_send, pair_recv,
           line_recv, up_send, down_send,
           lring_send, lring_recv, lpair_send, lpair_recv, lown_sem, out_sem):
    rows, basis = ints.shape
    chunks = fac.shape[0]
    half_rows = rows // 2
    spread = left.shape[1]
    sets = spread // 2
    row_blocks = rows // BLOCK
    col_blocks = basis // BLOCK
    bas_me = lax.axis_index("bas")
    z = lax.axis_index("aux")
    core = bas_me % 2
    half_ring = groups // 2

    def swap(index):
        upper = index // half_ring
        return index + upper * (3 * half_ring - 1 - 2 * index)

    pos = swap(bas_me // 2)

    def device_at(position, which):
        return 2 * swap(position % groups) + which

    partner = bas_me - core + (1 - core)

    def ring_to(half):
        return device_at(pos + groups + 1 - 2 * half, core)

    def remote(src, dst, send, recv, bas=None, aux_to=None):
        return pltpu.make_async_remote_copy(
            src_ref=src, dst_ref=dst, send_sem=send, recv_sem=recv,
            device_id={"bas": bas_me if bas is None else bas, "aux": z if aux_to is None else aux_to},
            device_id_type=pl.DeviceIdType.MESH)

    finish = []

    load_groups = 8
    load_cols = basis // load_groups

    def int_load(i):
        cols = pl.ds(i * load_cols, load_cols)
        return pltpu.make_async_copy(integrals.at[0, :, cols], ints.at[:, cols], load_sem.at[chunks + i])

    def fac_load(j):
        return pltpu.make_async_copy(coefs.at[:, pl.ds(j * LANES, LANES)], fac.at[j, bas_me], load_sem.at[j])

    for j in range(chunks):
        fac_load(j).start()
    for i in range(load_groups):
        int_load(i).start()

    barrier = pltpu.get_barrier_semaphore()
    for other in (ring_to(0), ring_to(1), partner):
        pl.semaphore_signal(barrier, inc=1, device_id={"bas": other, "aux": z}, device_id_type=pl.DeviceIdType.MESH)

    @pl.when(z > 0)
    def _():
        pl.semaphore_signal(barrier, inc=1, device_id={"bas": bas_me, "aux": z - 1}, device_id_type=pl.DeviceIdType.MESH)

    @pl.when(z < aux - 1)
    def _():
        pl.semaphore_signal(barrier, inc=1, device_id={"bas": bas_me, "aux": z + 1}, device_id_type=pl.DeviceIdType.MESH)

    peers = 3 + (z + aux - 1) // aux + (2 * aux - 2 - z) // aux
    pl.semaphore_wait(barrier, peers)

    def origin(h, half, which):
        return device_at(pos + groups - h + 2 * h * half, which)

    def fac_piece(j, h, half, which):
        return fac.at[j, origin(h, half, which), pl.ds(half * half_rows, half_rows)]

    def ring_copy(j, h, half):
        piece = fac_piece(j, h, half, core)
        return remote(piece, piece, ring_send.at[j, h, half], ring_recv.at[j, h, half], bas=ring_to(half))

    def pair_copy(j, h, half):
        piece = fac_piece(j, h, half, core)
        return remote(piece, piece, pair_send.at[j, h, half], pair_recv.at[j, h, half], bas=partner)

    def pass_on(j, h, half):
        if h < groups - 1:
            ring_copy(j, h, half).start()
            finish.append(ring_copy(j, h, half).wait_send)
        pair_copy(j, h, half).start()
        finish.append(pair_copy(j, h, half).wait_send)

    def ring_own(j):
        fac_load(j).wait()
        for half in (0, 1):
            pass_on(j, 0, half)

    def ring_step(j, h):
        for half in (0, 1):
            piece = fac_piece(j, h, half, core)
            remote(piece, piece, ring_send.at[j, h - 1, half], ring_recv.at[j, h - 1, half], bas=ring_to(half)).wait_recv()
            pass_on(j, h, half)

    def pair_wait(j, h):
        for half in (0, 1):
            piece = fac_piece(j, h, half, 1 - core)
            remote(piece, piece, pair_send.at[j, h, half], pair_recv.at[j, h, half], bas=partner).wait_recv()

    def mask_group(i):
        int_load(i).wait()
        per = col_blocks // load_groups

        def body(q, carry):
            column = i * per + q
            cols = pl.ds(pl.multiple_of(column * BLOCK, BLOCK), BLOCK)
            for r in range(row_blocks):
                keep = screen[0, r, column].astype(jnp.float32)
                keep = jnp.full((BLOCK, BLOCK), keep, jnp.float32).astype(jnp.bfloat16)
                ints[pl.ds(r * BLOCK, BLOCK), cols] = ints[pl.ds(r * BLOCK, BLOCK), cols] * keep
            return carry

        lax.fori_loop(0, per, body, 0)

    tile_m = min(256, rows)
    fine = half_rows % LANES == 0

    def piece_dot(j, block, start, length, first):
        def body(m, carry):
            at = pl.ds(pl.multiple_of(m * tile_m, tile_m), tile_m)
            cols = pl.ds(pl.multiple_of(block * rows + start, LANES), length)
            part = jnp.dot(ints[at, cols], fac[j, block, pl.ds(start, length), :],
                           preferred_element_type=jnp.float32)
            acc[j, at, :] = part if first else acc[j, at, :] + part
            return carry

        lax.fori_loop(0, rows // tile_m, body, 0)

    def half_dots(j, h):
        pair_wait(j, h)
        if fine:
            if h == 0:
                piece_dot(j, bas_me, 0, rows, True)
                piece_dot(j, partner, 0, rows, False)
            else:
                for half in (0, 1):
                    for which in (core, 1 - core):
                        piece_dot(j, origin(h, half, which), half * half_rows, half_rows, False)
        elif h == groups - 1:
            acc[j] = jnp.zeros(acc.shape[1:], acc.dtype)

            def body(block, carry):
                piece_dot(j, block, 0, rows, False)
                return carry

            lax.fori_loop(0, 2 * groups, body, 0)

    def weigh(j, p):
        values = right[j, p].astype(jnp.float32) * weights[:, pl.ds(j * LANES, LANES)]
        wt[j, pl.ds(pl.multiple_of(p * LANES, LANES), LANES), :] = values.T.astype(jnp.bfloat16)

    def up_copy(j, p):
        return remote(right.at[j, p], right.at[j, p], up_send.at[j, p], line_recv.at[j, p], aux_to=z + 1)

    def down_copy(j, p):
        return remote(right.at[j, p], right.at[j, p], down_send.at[j, p], line_recv.at[j, p], aux_to=z - 1)

    def guard(condition, action):
        pl.when(condition)(lambda: action())

    def send_up(j, p, condition):
        condition = condition & (z < aux - 1)
        guard(condition, lambda: up_copy(j, p).start())
        finish.append(lambda: guard(condition, lambda: up_copy(j, p).wait_send()))

    def send_down(j, p, condition):
        condition = condition & (z > 0)
        guard(condition, lambda: down_copy(j, p).start())
        finish.append(lambda: guard(condition, lambda: down_copy(j, p).wait_send()))

    def left_piece(ref_index, half):
        j, s, p = ref_index
        return left.at[j, s, p, pl.ds(half * half_rows, half_rows)]

    def lring_copy(src, j, t, p, half):
        return remote(src, left_piece((j, 2 * t + core, p), half),
                      lring_send.at[j, t, p, half], lring_recv.at[j, t, p, half], bas=ring_to(half))

    def lpair_copy(src, j, t, p, half):
        return remote(src, left_piece((j, 2 * t + core, p), half),
                      lpair_send.at[j, t, p, half], lpair_recv.at[j, t, p, half], bas=partner)

    def lown_copy(j, t, p):
        return pltpu.make_async_copy(right.at[j, p], left.at[j, 2 * t + core, p], lown_sem.at[j, t, p])

    def away(t):
        return (pos - swap(z * sets + t) + groups) % groups

    def left_start(j, p, condition):
        for t in range(sets):
            mine = condition & (away(t) == 0)

            def go(t=t):
                for half in (0, 1):
                    src = right.at[j, p, pl.ds(half * half_rows, half_rows)]
                    lring_copy(src, j, t, p, half).start()
                    lpair_copy(src, j, t, p, half).start()
                lown_copy(j, t, p).start()

            def end(t=t):
                for half in (0, 1):
                    src = right.at[j, p, pl.ds(half * half_rows, half_rows)]
                    lring_copy(src, j, t, p, half).wait_send()
                    lpair_copy(src, j, t, p, half).wait_send()

            guard(mine, go)
            finish.append(lambda mine=mine, end=end: guard(mine, end))

    def left_stage(j, p, condition, stage):
        for t in range(sets):
            distance = away(t)
            side = (2 * distance) // (groups + 1)
            middle = distance == half_ring
            other = condition & (distance != 0)
            takes = other & (middle if stage == 1 else distance != half_ring)
            halves = (0, 1) if stage == 1 else (side if stage == 0 else 1 - side,)
            for half in halves:
                hops = distance + half * (groups - 2 * distance)
                src = left_piece((j, 2 * t + core, p), half)

                def go(t=t, half=half, src=src):
                    lring_copy(src, j, t, p, half).wait_recv()
                    lpair_copy(src, j, t, p, half).start()

                def onward(t=t, half=half, src=src):
                    lring_copy(src, j, t, p, half).start()

                def end(t=t, half=half, src=src):
                    lpair_copy(src, j, t, p, half).wait_send()

                def end_onward(t=t, half=half, src=src):
                    lring_copy(src, j, t, p, half).wait_send()

                further = takes & (hops < groups - 1)
                guard(takes, go)
                guard(further, onward)
                finish.append(lambda takes=takes, end=end: guard(takes, end))
                finish.append(lambda further=further, end=end_onward: guard(further, end))

    def left_close(j, p, condition):
        for t in range(sets):
            mine = condition & (away(t) == 0)

            def own(t=t):
                lown_copy(j, t, p).wait()

            guard(mine, own)

            def from_partner(t=t):
                for half in (0, 1):
                    dst = left_piece((j, 2 * t + 1 - core, p), half)
                    remote(dst, dst, lpair_send.at[j, t, p, half], lpair_recv.at[j, t, p, half], bas=partner).wait_recv()

            guard(condition, from_partner)

    always = z >= 0

    def members(d):
        if d == 0:
            return [(z, always)]
        return [(z - d, z - d >= 0), (z + d, z + d < aux)]

    def line_event(j, d):
        for p, there in members(d):
            if d == 0:
                send_up(j, p, there)
                send_down(j, p, there)
            elif p is not None:
                guard(there, lambda p=p: up_copy(j, p).wait_recv())
        if d > 0:
            below, above = members(d)
            send_up(j, below[0], below[1])
            send_down(j, above[0], above[1])
        for p, there in members(d):
            left_start(j, p, there)
        if d > 0:
            for p, there in members(d):
                guard(there, lambda p=p: weigh(j, p))

    def close_half(j):
        right[j, z] = acc[j].astype(jnp.bfloat16)
        weigh(j, z)
        slot((j, 0))

    tile_n = min(256, rows)
    tiles_in = rows // tile_n
    tiles = spread * tiles_in

    def out_copy(i):
        at = pl.ds(i * tile_n, tile_n)
        return pltpu.make_async_copy(result.at[at], out.at[at], out_sem.at[i])

    def exchange(j, low, high):
        def body(i, carry):
            s, r = i // tiles_in, i % tiles_in
            at = pl.ds(pl.multiple_of(r * tile_n, tile_n), tile_n)
            lhs = jnp.concatenate([left[j, s, p, at, :] for p in range(aux)], axis=1)
            part = jnp.dot(lhs, wt[j], preferred_element_type=jnp.float32)
            to = pl.ds(pl.multiple_of(i * tile_n, tile_n), tile_n)
            if j > 0:
                part = total[to, :] + part
            if j == chunks - 1:
                result[to, :] = (part * scale).astype(jnp.bfloat16)
            else:
                total[to, :] = part
            return carry

        lax.fori_loop(low, high, body, 0)

    ran = []
    closed = [0] * chunks
    work = []

    def slot(event):
        if event is not None:
            line_event(*event)
        ran.append(event)
        n = len(ran) - 1
        for stage in range(3):
            if 0 <= n - 1 - stage and ran[n - 1 - stage] is not None:
                j, d = ran[n - 1 - stage]
                for p, there in members(d):
                    left_stage(j, p, there, stage)
        if n >= 4 and ran[n - 4] is not None:
            j, d = ran[n - 4]
            for p, there in members(d):
                left_close(j, p, there)
            closed[j] += 1
            if closed[j] == aux and j < chunks - 1:
                step = -(-tiles // max(1, aux - 1))
                work.extend((j, low, min(tiles, low + step)) for low in range(0, tiles, step))

    events = [(j, d) for j in range(chunks) for d in range(1, aux)]
    ring_own(0)
    if chunks > 1:
        ring_own(1)
    for i in range(load_groups // 2):
        mask_group(i)
    ring_step(0, 1)
    for i in range(load_groups // 2, load_groups):
        mask_group(i)
    for h in range(1, groups - 1):
        if h > 1:
            ring_step(0, h)
        half_dots(0, h - 1)
        if chunks > 1:
            ring_step(1, h)
            half_dots(1, h - 1)
    if groups > 2:
        ring_step(0, groups - 1)
    if chunks > 2:
        ring_own(2)
    half_dots(0, groups - 2)
    half_dots(0, groups - 1)
    close_half(0)
    if chunks > 1:
        ring_step(1, groups - 1)
        half_dots(1, groups - 2)
        half_dots(1, groups - 1)
        close_half(1)
    for j in range(2, chunks):
        for h in range(1, groups):
            ring_step(j, h)
            half_dots(j, h - 1)
            if h in (half_ring, groups - 1) and events and events[0][0] < j - 1:
                slot(events.pop(0))
        if j + 1 < chunks:
            ring_own(j + 1)
        half_dots(j, groups - 1)
        close_half(j)
    for event in events:
        slot(event)
        if work:
            exchange(*work.pop(0))
    for _ in range(4):
        if work:
            exchange(*work.pop(0))
        slot(None)
    for item in work:
        exchange(*item)
    parts = 4 if tiles % 4 == 0 else 1
    for i in range(parts):
        low, high = i * tiles // parts, (i + 1) * tiles // parts
        exchange(chunks - 1, low, high)
        if i > 0:
            for n in range((i - 1) * tiles // parts, low):
                out_copy(n).start()
    for n in range((parts - 1) * tiles // parts, tiles):
        out_copy(n).start()
    for action in finish:
        action()
    for n in range(tiles):
        out_copy(n).wait()


def shards(integrals, screen, coefficients, weights):
    _, rows, basis = integrals.shape
    occ = coefficients.shape[1]
    bas, aux = lax.axis_size("bas"), lax.axis_size("aux")
    groups, spread, chunks = bas // 2, bas // aux, occ // LANES
    sets = spread // 2
    tiles = spread * rows // min(256, rows)
    scale = 1.0 / math.sqrt(integrals.shape[0] * aux * occ)
    dma = pltpu.SemaphoreType.DMA
    bf16, f32 = jnp.bfloat16, jnp.float32
    return pl.pallas_call(
        functools.partial(kernel, groups, aux, scale),
        out_shape=jax.ShapeDtypeStruct((spread * rows, rows), bf16),
        in_specs=[
            pl.BlockSpec(memory_space=pl.ANY),
            pl.BlockSpec(memory_space=pltpu.SMEM),
            pl.BlockSpec(memory_space=pl.ANY),
            pl.BlockSpec(memory_space=pltpu.VMEM),
        ],
        out_specs=pl.BlockSpec(memory_space=pl.ANY),
        scratch_shapes=[
            pltpu.VMEM((rows, basis), bf16),
            pltpu.VMEM((chunks, bas, rows, LANES), bf16),
            pltpu.VMEM((chunks, rows, LANES), f32),
            pltpu.VMEM((chunks, aux, rows, LANES), bf16),
            pltpu.VMEM((chunks, spread, aux, rows, LANES), bf16),
            pltpu.VMEM((chunks, aux * LANES, rows), bf16),
            pltpu.VMEM((spread * rows, rows), f32),
            pltpu.VMEM((spread * rows, rows), bf16),
            dma((chunks + 8,)),
            dma((chunks, groups, 2)), dma((chunks, groups, 2)),
            dma((chunks, groups, 2)), dma((chunks, groups, 2)),
            dma((chunks, aux)), dma((chunks, aux)), dma((chunks, aux)),
            dma((chunks, sets, aux, 2)), dma((chunks, sets, aux, 2)),
            dma((chunks, sets, aux, 2)), dma((chunks, sets, aux, 2)),
            dma((chunks, sets, aux)),
            dma((tiles,)),
        ],
        compiler_params=pltpu.CompilerParams(
            collective_id=0, has_side_effects=True, vmem_limit_bytes=62 * 1024 * 1024),
    )(integrals, screen, coefficients, weights.reshape(1, occ))


def solution(mesh):
    in_specs = (P("aux", "bas", None), P("aux", "bas", None), P("bas", None), P())
    out_specs = P("aux", "bas")
    return jax.shard_map(shards, mesh=mesh, in_specs=in_specs, out_specs=out_specs, check_vma=False)
```

profile of v0, /device:TPU:3, one launch (start us, length us, event | category | flops | bytes accessed | tf_op | source)
XLA Modules:
  0.0 115.4 jit_solution(17354251755322563039)
XLA Ops:
  0.0 1.2 %reshape.3.weights = f32[1,384]{1,0:T(1,128)} reshape(f32[384]{0:T(512)} %param.7) | data formatting | bytes 3072 | tf_op jit(solution)/shard_map/reshape | solution.py:457
  1.2 109.5 %shard_map.46 = bf16[2048,1024]{1,0:T(8,128)(2,1)} custom-call(bf16[1,1024,8192]{2,1,0:T(8,128)(2,1)} %integrals.1, s32[1,8,64]{2,1,0:T(8,128)} %screen.1, bf16[1024,384]{1,0:T(8,128)(2,1)} %coefs.1, f32[1,384]{1,0:T(1,128)} %reshape.3.weights), custom_call_target="tpu_custom_call" | custom-call | tf_op jit(solution)/shard_map/pallas_call | solution.py:427
  110.7 4.6 %copy.6 = bf16[2048,1024]{1,0:T(8,128)(2,1)} copy(bf16[2048,1024]{1,0:T(8,128)(2,1)} %shard_map.46) | data formatting | bytes 8388608
where the time goes:
time: 116 us; the launch traced here: 115 us
  Pallas kernels  109 us (94%)
  local copies, waits for them, and re-layouts  5.89 us (5%)
    pallas_call x1, Pallas kernels, shards(): pl.pallas_call(functools.partial(kernel, groups, aux, scale), out_shape=j...  109 us
    unnamed x1, local copies, waits for them, and re-layouts  4.64 us

commit v1 on v0

v1 whole, which is shorter than its diff:
```python
import functools
import math

import jax
import jax.numpy as jnp
from jax import lax
from jax.experimental import pallas as pl
from jax.experimental.pallas import tpu as pltpu
from jax.sharding import PartitionSpec as P

BLOCK = 128
LANES = 128


def scoped(name):
    def wrap(call):
        return call
    return wrap


ZINT = 5.66
OWN = (2.0, 9.7, 26.5)
DOTS = (8.0, 16.6, 40.3)
PACE = (0.8, 1.0, 1.4)
HALF = (16.5, 28.4, 54.4)
LINE = (19.3, 35.8, 60.7)
FIRST = (3.9, 7.5, 0.5)
HOP = (8.9, 7.2, 4.9)
LAST = (8.0, 1.0, 2.4)
WIDE = 1.4


def place(groups, i):
    hop, sub = (i + 2) // 4, (i + 2) % 4
    middle = 2 * hop // groups
    edge = 1 - (hop + groups - 1) // groups + middle
    side = (1 - middle) * (sub % 2)
    other = edge * (sub % 2) + (1 - edge) * (sub // 2)
    return hop + side * (groups - 2 * hop), other


def plan(groups, aux, pieces, stages, tiles, early):
    chunks, bas = len(pieces), 2 * groups
    timed = []

    def at(time, *op):
        timed.append((time, len(timed), op))

    def when(table, j):
        return table[min(j, len(table) - 1)] + max(0, j - len(table) + 1) * 3 * ZINT

    for j in range(chunks):
        if j > 0:
            at(when(OWN, j), "own", j)
        for i in range(bas):
            offset, other = place(groups, i)
            offset = offset % groups
            hop = min(offset, groups - offset)
            time = when(DOTS, j) + PACE[min(j, 2)] * i * 8 / bas
            if other == 0 and offset == hop > 0:
                at(time - 0.003 - 100 * (j == 0 and hop == 1), "take", j, hop, 0)
                if 2 * hop < groups:
                    at(time - 0.002, "take", j, hop, 1)
            if other == 1:
                at(time - 0.001, "pair", j, offset)
            if j == 0 and i == early:
                at(-50, "late")
            if j == 0 and i >= early:
                at(time - 0.0005, "mask", i)
            at(time, "dot", j, i)
        at(when(HALF, j), "half", j)
        k = min(j, 2)
        for d in range(aux):
            for q in range(pieces[j]):
                if d == 0:
                    time = when(HALF, j) + 0.001
                    begin = time + FIRST[k] + q // 2 * ZINT / pieces[j] * WIDE
                    end = time + FIRST[k] + 3 * HOP[k] + LAST[k]
                else:
                    time = when(LINE, j) + ZINT * (d - 1 + q / pieces[j])
                    begin = time + FIRST[k]
                    end = begin + 2 * HOP[k] + LAST[k]
                at(time, "line", j, d, q)
                for s in range(stages):
                    at(begin + HOP[k] * s + 0.0001, "stage", j, d, q, s)
                at(end + 0.0001, "close", j, d, q)
    times = {op: time for time, _, op in timed}
    needs = []
    for j in range(chunks):
        if j > 0:
            needs += [(("own", j), ("take", j, 1, 0)), (("own", j), ("dot", j, 0)), (("half", j - 1), ("dot", j, 0)),
                      (("take", j - 1, 1, 0), ("own", j))]
        for hop in range(1, groups // 2 + 1):
            needs += [(("take", j, hop, 0), ("take", j, hop, 1)), (("take", j, hop, 0), ("take", j, hop + 1, 0)),
                      (("take", j, hop, 1), ("take", j, hop + 1, 0))]
        for i in range(bas):
            offset, other = place(groups, i)
            offset = offset % groups
            hop = min(offset, groups - offset)
            needs += [(("take", j, hop, 0), ("dot", j, i)), (("take", j, hop, 1), ("dot", j, i))]
            if other == 1:
                needs.append((("pair", j, offset), ("dot", j, i)))
                needs += [(("take", j, hop, 0), ("pair", j, offset)), (("take", j, hop, 1), ("pair", j, offset))]
            if j == 0:
                needs += [(("mask", i), ("dot", 0, i)), (("late",), ("mask", i))]
            needs.append((("dot", j, i), ("dot", j, i + 1) if i + 1 < bas else ("half", j)))
        for q in range(pieces[j - 1] if j > 0 else 0):
            needs += [(("close", j - 1, d, q), ("close", j, aux - 1, 0)) for d in range(aux)]
        for q in range(pieces[j]):
            if j == chunks - 1 and aux > 1:
                needs += [(("line", j, d, q), ("close", j, aux - 1, 0)) for d in range(aux)]
                needs += [(("close", j, d, q), ("close", j, aux - 1, q)) for d in range(aux - 1)]
            needs.append((("half", j), ("line", j, 0, q)))
            for d in range(1, aux):
                needs += [(("line", j, 0, own), ("line", j, d, q)) for own in range(pieces[j])]
    needs = [(first, then) for first, then in needs if first in times and then in times]
    moved = True
    while moved:
        moved = False
        for first, then in needs:
            if times[first] > times[then] - 0.00001:
                times[first] = times[then] - 0.00002
                moved = True
    order = sorted(times, key=lambda op: times[op])

    steps, waiting, closed = [], [], [0] * chunks
    for op in order:
        steps.append(op)
        if op[0] == "close":
            j, d, q = op[1:]
            closed[j] += 1
            if closed[j] == aux * pieces[j] and j < chunks - 1:
                waiting += [("exchange", j, low, min(tiles, low + 2)) for low in range(0, tiles, 2)]
            if j == chunks - 1 and d == aux - 1:
                if q == 0:
                    steps[-1:] = waiting + steps[-1:]
                    waiting = []
                steps.append(("final", q))
        if op[0] == "line" and waiting:
            steps.append(waiting.pop(0))
    return steps


def kernel(groups, aux, scale, integrals, screen, coefs, weights, out,
           ints, fac, acc, right, left, wt, total, result, keep,
           load_sem, ring_send, ring_recv, pair_send, pair_recv,
           line_recv, up_send, down_send,
           lring_send, lring_recv, lpair_send, lpair_recv, lown_sem, out_sem):
    rows, basis = integrals.shape[1:]
    chunks = fac.shape[0]
    half_rows = rows // 2
    spread = left.shape[1]
    sets = spread // 2
    row_blocks = rows // BLOCK
    bas = 2 * groups
    bas_me = lax.axis_index("bas")
    z = lax.axis_index("aux")
    core = bas_me % 2
    half_ring = groups // 2
    last = chunks - 1

    def swap(index):
        upper = index // half_ring
        return index + upper * (3 * half_ring - 1 - 2 * index)

    pos = swap(bas_me // 2)

    def device_at(position, which):
        return 2 * swap(position % groups) + which

    partner = bas_me - core + (1 - core)

    def ring_to(side):
        return device_at(pos + groups + 1 - 2 * side, core)

    def origin(offset, which):
        return device_at(pos + groups - offset, which)

    def remote(src, dst, send, recv, bas=None, aux_to=None):
        return pltpu.make_async_remote_copy(
            src_ref=src, dst_ref=dst, send_sem=send, recv_sem=recv,
            device_id={"bas": bas_me if bas is None else bas, "aux": z if aux_to is None else aux_to},
            device_id_type=pl.DeviceIdType.MESH)

    finish = {}

    def guard(condition, action):
        pl.when(condition)(lambda: action())

    def device_of(i):
        offset, other = place(groups, i)
        return device_at(pos + groups - offset, (core + other) % 2)

    def int_load(i):
        device = device_of(i)
        cols = pl.ds(pl.multiple_of(device * rows, LANES), rows)
        return pltpu.make_async_copy(integrals.at[0, :, cols], ints.at[device, :, pl.ds(0, rows)], load_sem.at[chunks + i])

    def fac_load(j):
        return pltpu.make_async_copy(coefs.at[:, pl.ds(j * LANES, LANES)], fac.at[j, bas_me], load_sem.at[j])

    for j in range(chunks):
        fac_load(j).start()

    early = bas // 2
    for i in range(early):
        int_load(i).start()

    barrier = pltpu.get_barrier_semaphore()
    for other in (ring_to(0), ring_to(1), partner):
        pl.semaphore_signal(barrier, inc=1, device_id={"bas": other, "aux": z}, device_id_type=pl.DeviceIdType.MESH)

    @pl.when(z > 0)
    def _():
        pl.semaphore_signal(barrier, inc=1, device_id={"bas": bas_me, "aux": z - 1}, device_id_type=pl.DeviceIdType.MESH)

    @pl.when(z < aux - 1)
    def _():
        pl.semaphore_signal(barrier, inc=1, device_id={"bas": bas_me, "aux": z + 1}, device_id_type=pl.DeviceIdType.MESH)

    peers = 3 + (z + aux - 1) // aux + (2 * aux - 2 - z) // aux

    @scoped("expand")
    def expand():
        flags = screen[0].astype(jnp.float32)
        wide = jnp.concatenate(
            [jnp.broadcast_to(flags[r:r + 1], (16, flags.shape[1])) for r in range(row_blocks)], axis=0)
        wide = wide.astype(jnp.bfloat16)
        span = basis // 8

        def body(q, carry):
            block = (lax.broadcasted_iota(jnp.int32, (flags.shape[1], span), 1) // BLOCK) + q * (span // BLOCK)
            here = block == lax.broadcasted_iota(jnp.int32, (flags.shape[1], span), 0)
            pick = jnp.where(here, 1.0, 0.0).astype(jnp.bfloat16)
            values = jnp.dot(wide, pick, preferred_element_type=jnp.float32)
            keep[:, pl.ds(pl.multiple_of(q * span, LANES), span)] = values.astype(jnp.bfloat16)
            return carry

        lax.fori_loop(0, 8, body, 0)

    @scoped("barrier")
    def enter():
        pl.semaphore_wait(barrier, peers)

    enter()

    def fac_piece(j, offset, half, which):
        return fac.at[j, origin(offset, which), pl.ds(half * half_rows, half_rows)]

    def reaches(hop, side):
        if 2 * hop < groups:
            return (side, 1 - side)
        return (side,) if 2 * hop == groups else ()

    def shift(hop, side):
        return hop if side == 0 else (groups - hop) % groups

    def ring_copy(j, side, hop, half):
        piece = fac_piece(j, shift(hop - 1, side), half, core)
        at = (j, side, hop - 1, half)
        return remote(piece, piece, ring_send.at[at], ring_recv.at[at], bas=ring_to(side))

    def ring_arrival(j, side, hop, half):
        piece = fac_piece(j, shift(hop, side), half, core)
        at = (j, side, hop - 1, half)
        return remote(piece, piece, ring_send.at[at], ring_recv.at[at], bas=ring_to(side))

    def pair_copy(j, offset, half, which):
        piece = fac_piece(j, offset, half, which)
        at = (j, offset, half)
        return remote(piece, piece, pair_send.at[at], pair_recv.at[at], bas=partner)

    def send_ring(j, side, hop, half):
        ring_copy(j, side, hop, half).start()
        finish["ring", j, side, hop, half] = lambda: ring_copy(j, side, hop, half).wait_send()

    def send_pair(j, offset, half):
        pair_copy(j, offset, half, core).start()
        finish["pair", j, offset, half] = lambda: pair_copy(j, offset, half, core).wait_send()

    @scoped("ring_own")
    def ring_own(j):
        fac_load(j).wait()
        for turn in (0, 1):
            for side in (0, 1):
                if turn < len(reaches(1, side)):
                    send_ring(j, side, 1, reaches(1, side)[turn])
        for half in (0, 1):
            send_pair(j, 0, half)

    @scoped("ring_take")
    def ring_take(j, hop, turn):
        for side in (0, 1):
            if turn < len(reaches(hop, side)):
                half = reaches(hop, side)[turn]
                ring_arrival(j, side, hop, half).wait_recv()
                if half in reaches(hop + 1, side):
                    send_ring(j, side, hop + 1, half)
                send_pair(j, shift(hop, side), half)

    def pair_wait(j, offset):
        for half in (0, 1):
            pair_copy(j, offset, half, 1 - core).wait_recv()

    @scoped("mask")
    def mask(i):
        int_load(i).wait()
        device = device_of(i)
        first = device * (rows // BLOCK)

        def body(q, carry):
            flags = pl.ds(pl.multiple_of((first + q) * BLOCK, BLOCK), BLOCK)
            cols = pl.ds(pl.multiple_of(q * BLOCK, BLOCK), BLOCK)
            for r in range(row_blocks):
                flag = keep[pl.ds(r * 16, 16), flags]
                for a in range(BLOCK // 16):
                    at = pl.ds(r * BLOCK + a * 16, 16)
                    ints[device, at, cols] = ints[device, at, cols] * flag
            return carry

        lax.fori_loop(0, rows // BLOCK, body, 0, unroll=2)

    pieces = [2] * last + [4]

    def span_of(j, q):
        return pl.ds(q * (rows // pieces[j]), rows // pieces[j])

    def member(d, side):
        if side == 0:
            return z - d, z >= d
        return z + d, z + d < aux

    def sides(d):
        return (0,) if d == 0 else (0, 1)

    def weigh(j, p, q):
        values = right[j, p, span_of(j, q)].astype(jnp.float32) * weights[:, pl.ds(j * LANES, LANES)]
        wt[j, pl.ds(pl.multiple_of(p * LANES, LANES), LANES), span_of(j, q)] = values.T.astype(jnp.bfloat16)

    def line_piece(j, p, q):
        return right.at[j, p, span_of(j, q)]

    def line_copy(j, p, q, to):
        piece = line_piece(j, p, q)
        sem = (down_send, up_send)[to]
        return remote(piece, piece, sem.at[j, p, q], line_recv.at[j, p, q], aux_to=z - 1 + 2 * to)

    def line_send(j, d, side, q, to):
        def on(action):
            p, there = member(d, side)
            room = (z < aux - 1) if to else (z > 0)
            guard(there & room, lambda: action(line_copy(j, p, q, to)))

        on(lambda copy: copy.start())
        finish["line", j, d, side, q, to] = lambda: on(lambda copy: copy.wait_send())

    def left_piece(j, s, p, q):
        return left.at[j, s, p, span_of(j, q)]

    def lring_copy(src, j, t, p, q):
        at = (j, t, p, q)
        return remote(src, left_piece(j, 2 * t + core, p, q), lring_send.at[at], lring_recv.at[at], bas=ring_to(q % 2))

    def lpair_copy(src, j, t, p, q):
        at = (j, t, p, q)
        return remote(src, left_piece(j, 2 * t + core, p, q), lpair_send.at[at], lpair_recv.at[at], bas=partner)

    def lown_copy(j, t, p, q):
        return pltpu.make_async_copy(line_piece(j, p, q), left_piece(j, 2 * t + core, p, q), lown_sem.at[j, t, p, q])

    def away(t):
        return (pos - swap(z * sets + t) + groups) % groups

    def left_start(j, d, side, q):
        for t in range(sets):
            def on(action, t=t):
                p, there = member(d, side)
                guard(there & (away(t) == 0), lambda: action(line_piece(j, p, q), j, t, p, q))

            def go(src, j, t, p, q):
                lring_copy(src, j, t, p, q).start()
                lpair_copy(src, j, t, p, q).start()
                lown_copy(j, t, p, q).start()

            def end(src, j, t, p, q):
                lring_copy(src, j, t, p, q).wait_send()
                lpair_copy(src, j, t, p, q).wait_send()

            on(go)
            finish["left", j, d, side, q, t] = lambda on=on, end=end: on(end)

    stages = min(3, groups - 1)

    def left_stage(j, d, side, q, stage):
        for t in range(sets):
            def on(action, onward, t=t):
                p, there = member(d, side)
                distance = away(t)
                hops = distance if q % 2 == 0 else groups - distance
                takes = there & (distance != 0) & ((stages * (hops - 1)) // max(1, groups - 1) == stage)
                if onward:
                    takes = takes & (hops < groups - 1)
                guard(takes, lambda: action(left_piece(j, 2 * t + core, p, q), j, t, p, q))

            on(lambda *a: lring_copy(*a).wait_recv(), False)
            on(lambda *a: lring_copy(*a).start(), True)
            on(lambda *a: lpair_copy(*a).start(), False)

            def end(on=on):
                on(lambda *a: lpair_copy(*a).wait_send(), False)
                on(lambda *a: lring_copy(*a).wait_send(), True)

            finish["stage", j, d, side, q, stage, t] = end

    def left_close(j, d, side, q):
        p, there = member(d, side)
        for t in range(sets):
            guard(there & (away(t) == 0), lambda t=t: lown_copy(j, t, p, q).wait())

            def from_partner(t=t):
                dst = left_piece(j, 2 * t + 1 - core, p, q)
                at = (j, t, p, q)
                remote(dst, dst, lpair_send.at[at], lpair_recv.at[at], bas=partner).wait_recv()

            guard(there, from_partner)

    @scoped("line")
    def line_event(j, d, q):
        for side in sides(d):
            if d == 0:
                line_send(j, d, side, q, 1)
                line_send(j, d, side, q, 0)
            else:
                p, there = member(d, side)
                guard(there, lambda p=p: line_copy(j, p, q, 1).wait_recv())
                line_send(j, d, side, q, 1 - side)
        for side in sides(d):
            left_start(j, d, side, q)
        for side in sides(d):
            p, there = member(d, side)
            guard(there, lambda p=p: weigh(j, p, q))

    tile_n = min(256, rows // 4)
    tiles_in = rows // tile_n
    tiles = spread * tiles_in

    def out_copy(i):
        at = pl.ds(i * tile_n, tile_n)
        return pltpu.make_async_copy(result.at[at], out.at[at], out_sem.at[i])

    def tile(j, s, r):
        at = pl.ds(pl.multiple_of(r * tile_n, tile_n), tile_n)
        lhs = jnp.concatenate([left[j, s, p, at, :] for p in range(aux)], axis=1)
        to = pl.ds(pl.multiple_of((s * tiles_in + r) * tile_n, tile_n), tile_n)
        if j > 0:
            part = total[to, :] + jnp.dot(lhs, wt[j], preferred_element_type=jnp.float32)
        else:
            part = jnp.dot(lhs, wt[j], preferred_element_type=jnp.float32)
        if j == last:
            result[to, :] = (part * scale).astype(jnp.bfloat16)
        else:
            total[to, :] = part

    @scoped("exchange")
    def exchange(j, low, high):
        def body(i, carry):
            tile(j, i // tiles_in, i % tiles_in)
            return carry

        lax.fori_loop(low, high, body, 0)

    @scoped("final")
    def final(q):
        per = tiles_in // pieces[last]

        def body(i, carry):
            tile(last, i // per, q * per + i % per)
            return carry

        lax.fori_loop(0, spread * per, body, 0)
        for s in range(spread):
            for r in range(q * per, q * per + per):
                out_copy(s * tiles_in + r).start()

    @scoped("late")
    def late():
        for i in range(early, bas):
            int_load(i).start()

    @scoped("half")
    def close_half(j):
        right[j, z] = acc[j].astype(jnp.bfloat16)

    def stage(j, d, q, s):
        for side in sides(d):
            left_stage(j, d, side, q, s)

    def close(j, d, q):
        for side in sides(d):
            left_close(j, d, side, q)

    kinds = {"own": ring_own, "take": ring_take, "pair": pair_wait, "late": late, "mask": mask, "half": close_half,
             "line": line_event, "stage": stage, "close": close, "exchange": exchange, "final": final}

    def do(op):
        kinds[op[0]](*op[1:])

    steps = plan(groups, aux, pieces, stages, tiles, early)

    def chunk(j, ops):
        todo = {i: [] for i in range(bas)}
        i = 0
        for op in ops:
            if op[0] == "dot":
                i += 1
            else:
                todo[i].append(op)

        def body(i, carry):
            @pl.when(i == 0)
            def _():
                acc[j] = jnp.zeros(acc.shape[1:], acc.dtype)

            for k in range(bas):
                if todo[k]:
                    @pl.when(i == k)
                    def _(k=k):
                        for op in todo[k]:
                            do(op)

            device = device_of(i)
            acc[j] = acc[j] + jnp.dot(ints[device, :, pl.ds(0, rows)], fac[j, device], preferred_element_type=jnp.float32)
            return carry

        lax.fori_loop(0, bas, body, 0)

    ring_own(0)
    expand()
    for i in range(early):
        mask(i)
    n = 0
    while n < len(steps):
        op = steps[n]
        if op[0] == "dot":
            end = steps.index(("dot", op[1], bas - 1))
            chunk(op[1], steps[n:end + 1])
            n = end + 1
        else:
            do(op)
            n += 1
    for action in finish.values():
        action()
    for n in range(tiles):
        out_copy(n).wait()


def shards(integrals, screen, coefficients, weights):
    _, rows, basis = integrals.shape
    occ = coefficients.shape[1]
    bas, aux = lax.axis_size("bas"), lax.axis_size("aux")
    groups, spread, chunks = bas // 2, bas // aux, occ // LANES
    sets = spread // 2
    tiles = spread * rows // min(256, rows // 4)
    reach = max(1, groups // 2)
    scale = 1.0 / math.sqrt(integrals.shape[0] * aux * occ)
    dma = pltpu.SemaphoreType.DMA
    bf16, f32 = jnp.bfloat16, jnp.float32
    return pl.pallas_call(
        functools.partial(kernel, groups, aux, scale),
        out_shape=jax.ShapeDtypeStruct((spread * rows, rows), bf16),
        in_specs=[
            pl.BlockSpec(memory_space=pl.ANY),
            pl.BlockSpec(memory_space=pltpu.VMEM),
            pl.BlockSpec(memory_space=pl.ANY),
            pl.BlockSpec(memory_space=pltpu.VMEM),
        ],
        out_specs=pl.BlockSpec(memory_space=pl.ANY),
        scratch_shapes=[
            pltpu.VMEM((bas, rows, rows + LANES), bf16),
            pltpu.VMEM((chunks, bas, rows, LANES), bf16),
            pltpu.VMEM((chunks, rows, LANES), f32),
            pltpu.VMEM((chunks, aux, rows, LANES), bf16),
            pltpu.VMEM((chunks, spread, aux, rows, LANES), bf16),
            pltpu.VMEM((chunks, aux * LANES, rows), bf16),
            pltpu.VMEM((spread * rows, rows), f32),
            pltpu.VMEM((spread * rows, rows), bf16),
            pltpu.VMEM((rows // BLOCK * 16, basis), bf16),
            dma((chunks + bas,)),
            dma((chunks, 2, reach, 2)), dma((chunks, 2, reach, 2)),
            dma((chunks, groups, 2)), dma((chunks, groups, 2)),
            dma((chunks, aux, 4)), dma((chunks, aux, 4)), dma((chunks, aux, 4)),
            dma((chunks, sets, aux, 4)), dma((chunks, sets, aux, 4)),
            dma((chunks, sets, aux, 4)), dma((chunks, sets, aux, 4)),
            dma((chunks, sets, aux, 4)),
            dma((tiles,)),
        ],
        compiler_params=pltpu.CompilerParams(
            collective_id=0, has_side_effects=True, vmem_limit_bytes=62 * 1024 * 1024),
    )(integrals, screen, coefficients, weights.reshape(1, occ))


def solution(mesh):
    in_specs = (P("aux", "bas", None), P("aux", "bas", None), P("bas", None), P())
    out_specs = P("aux", "bas")
    return jax.shard_map(shards, mesh=mesh, in_specs=in_specs, out_specs=out_specs, check_vma=False)
```

time: 116 us -> 104 us (0.90)
  Pallas kernels: 109 us -> 97.8 us
    pallas_call x1, Pallas kernels: 109 us -> 97.8 us  [shards(): pl.pallas_call(functools.partial(kernel, groups, aux, scale), out_shape=j...]
where the time goes in v1:
time: 104 us
  Pallas kernels  97.8 us (94%)
  local copies, waits for them, and re-layouts  5.89 us (6%)
    pallas_call x1, Pallas kernels, shards(): pl.pallas_call(functools.partial(kernel, groups, aux, scale), out_shape=j...  97.8 us
    unnamed x1, local copies, waits for them, and re-layouts  4.64 us

profile of v1, /device:TPU:3, one launch (start us, length us, event | category | flops | bytes accessed | tf_op | source)
XLA Modules:
  0.0 103.7 jit_solution(12753606037270615676)
XLA Ops:
  0.0 1.2 %reshape.3.weights = f32[1,384]{1,0:T(1,128)} reshape(f32[384]{0:T(512)} %param.7) | data formatting | bytes 3072 | tf_op jit(solution)/shard_map/reshape | solution.py:599
  1.2 97.8 %shard_map.46 = bf16[2048,1024]{1,0:T(8,128)(2,1)} custom-call(bf16[1,1024,8192]{2,1,0:T(8,128)(2,1)} %integrals.1, s32[1,8,64]{2,1,0:T(8,128)} %screen.1, bf16[1024,384]{1,0:T(8,128)(2,1)} %coefs.1, f32[1,384]{1,0:T(1,128)} %reshape.3.weights), custom_call_target="tpu_custom_call" | custom-call | tf_op jit(solution)/shard_map/pallas_call | solution.py:568
  99.0 4.6 %copy.6 = bf16[2048,1024]{1,0:T(8,128)(2,1)} copy(bf16[2048,1024]{1,0:T(8,128)(2,1)} %shard_map.46) | data formatting | bytes 8388608
